TPU v7x, 32 devices: a whole 2x2x4 slice. The times are simulated.
32 devices in a mesh: parts: 2 (over y), expert: 16 (over z, x, core), dp: 1.
Axes of the slice: x: 2, y: 2, z: 4, core: 2. Of those that a mesh axis runs over, the one named last changes fastest.
Arguments:
- tokens: bfloat16 [2048, 2048], P(('parts', 'expert', 'dp')), parts along dimension 0, may hold values from -6 to 6
- expert_ids: int32 [2048, 8], P(('parts', 'expert', 'dp')), parts along dimension 0, may hold values from 0 to 15, all different within a row; in each aligned block of 64 rows (0 to 63, 64 to 127, ...) at most 64 rows name the same one
- router_weights: float32 [2048, 8], P(('parts', 'expert', 'dp')), parts along dimension 0, may hold values from 0.1 to 1
- w_gate: bfloat16 [16, 2048, 768], P('expert', None, 'dp'), may hold values from -0.125 to 0.125
- w_up: bfloat16 [16, 2048, 768], P('expert', None, 'dp'), may hold values from -0.125 to 0.125
- w_down: bfloat16 [16, 2048, 768], P('expert', None, 'dp'), may hold values from -0.21875 to 0.21875
Outputs:
- mixed: bfloat16 [2048, 2048], P(('parts', 'expert', 'dp')), parts along dimension 0
There are 2 independent parts, one for each index of `parts`. A program takes and returns all parts, laid end to end along the dimension named above; an argument that names none is the same for every part. Nothing has to cross between parts.
Inputs may be any that keep to these rules, and one draw needn't show every extreme that they name: `expert_ids`: each token names 8 different experts. Among the 64 tokens of one device no expert is named more than 64 times, and in every draw some expert is named exactly 64 times by the tokens of some device.
All inputs are finite; a program needn't handle non-finite values.
Results may differ from a plain program's by a relative error of at most 0.008.
Values may be sent and summed in bfloat16 or wider, within the bound.
A program may use at most 128 MiB of HBM per device.

v0:
```python
import math

import jax
import jax.numpy as jnp
from jax import lax
from jax.sharding import PartitionSpec as P


def expert_rows(rows, gate_w, up_w, down_w):
    total = rows.shape[0]
    block = math.gcd(total, 128)
    pieces = []
    for index in range(total // block):
        block_rows = rows[index * block : (index + 1) * block]
        gate_val = jnp.dot(block_rows, gate_w, preferred_element_type=jnp.float32)
        up_val = jnp.dot(block_rows, up_w, preferred_element_type=jnp.float32)
        hidden = (jax.nn.silu(gate_val) * up_val).astype(jnp.bfloat16)
        pieces.append(
            lax.dot_general(
                hidden, down_w, (((1,), (1,)), ((), ())), preferred_element_type=jnp.float32
            )
        )
    return jnp.concatenate(pieces, 0)


def body(tokens, expert_ids, router_weights, w_gate, w_up, w_down):
    tok_count, top = expert_ids.shape
    width = tokens.shape[1]
    experts = lax.axis_size("expert")
    cap = max(2, min(tok_count, 2 * tok_count * top // experts))
    slots_all = experts * cap
    flat_ids = expert_ids.reshape(-1)
    onehot = (flat_ids[:, None] == jnp.arange(experts, dtype=jnp.int32)[None, :]).astype(jnp.int32)
    before = jnp.cumsum(onehot, 0) - onehot
    position = jnp.sum(before * onehot, 1)
    slot = flat_ids * cap + position
    send = jnp.zeros((slots_all, width), jnp.bfloat16).at[slot].set(jnp.repeat(tokens, top, 0))
    send = send.reshape(experts, cap, width)
    arrived = lax.all_to_all(send, "expert", split_axis=0, concat_axis=0, tiled=True)
    packed = arrived.reshape(slots_all, width)
    result = expert_rows(
        packed,
        lax.all_gather(w_gate, "dp", axis=2, tiled=True)[0],
        lax.all_gather(w_up, "dp", axis=2, tiled=True)[0],
        lax.all_gather(w_down, "dp", axis=2, tiled=True)[0],
    )
    expert_out = result.astype(jnp.bfloat16)
    back = lax.all_to_all(
        expert_out.reshape(experts, cap, width), "expert", split_axis=0, concat_axis=0, tiled=True
    )
    picked = back.reshape(slots_all, width)[slot].reshape(tok_count, top, width)
    mixed = jnp.einsum("tk,tkd->td", router_weights, picked.astype(jnp.float32))
    return mixed.astype(jnp.bfloat16)


def solution(mesh):
    in_specs = (
        P(("parts", "expert", "dp"), None),
        P(("parts", "expert", "dp"), None),
        P(("parts", "expert", "dp"), None),
        P("expert", None, "dp"),
        P("expert", None, "dp"),
        P("expert", None, "dp"),
    )
    out_specs = P(("parts", "expert", "dp"), None)
    return jax.shard_map(body, mesh=mesh, in_specs=in_specs, out_specs=out_specs, check_vma=False)
```

profile of v0, /device:TPU:11, one launch (start us, length us, event | category | flops | bytes accessed | tf_op | source)
XLA Modules:
  0.0 267.4 jit_solution(9964746450724570678)
XLA Ops:
  0.0 0.0 copy-start
  0.0 0.9 copy.8
  0.9 0.1 eq.29
  1.0 0.1 eq.25
  1.1 0.7 broadcast_multiply_fusion
  1.8 1.1 reduce-window.6
  3.0 0.2 slice_reduce_fusion
  3.2 0.1 copy.7
  3.3 0.1 mul.70
  3.4 0.1 fusion.216
  3.5 6.6 %scatter_custom_fusion = bf16[1024,2048]{1,0:T(8,128)(2,1)} fusion(s32[512]{0:T(512)S(1)} %bitcast.208, bf16[]{:T(256)} %constant.18.clone.1, bf16[64,2048]{1,0:T(8,128)(2,1)} %param.6), kind=kCustom, calls=%fused_computation.68 | custom fusion | bytes 4456450 | tf_op jit(solution)/shard_map/scatter | solution.py:37
  10.1 98.7 %all_to_all.10 = bf16[16,64,2048]{2,1,0:T(8,128)(2,1)S(1)} all-to-all(bf16[16,64,2048]{2,1,0:T(8,128)(2,1)} %bitcast.190), channel_id=1, replica_groups=mesh['parts'=2,'expert'=16,'dp'=1] {'expert'}, dimensions={0} | all-to-all | bytes 8388608 | tf_op jit(solution)/shard_map/all_to_all | solution.py:39
  108.8 0.0 copy-start.1
  108.8 0.6 fusion.226
  109.4 0.0 copy-start.8
  109.4 0.0 copy-start.9
  109.4 0.0 copy-start.7
  109.4 0.0 copy-start.6
  109.4 0.0 copy-start.5
  109.4 0.0 copy-start.4
  109.5 0.0 copy-start.3
  109.5 0.0 copy-start.2
  109.5 2.1 copy-done.1
  111.6 1.4 fusion.46
  112.9 1.4 fusion.44
  114.3 0.0 copy-done.8
  114.3 0.0 copy-done.9
  114.3 0.0 copy-done.7
  114.3 1.3 fusion.42
  115.6 0.0 copy-done.6
  115.6 1.3 fusion.40
  117.0 0.0 copy-done.5
  117.0 1.4 fusion.38
  118.3 0.0 copy-done.4
  118.3 1.4 fusion.36
  119.7 0.0 copy-done.3
  119.7 1.4 fusion.34
  121.1 0.0 copy-done.2
  121.1 0.6 fusion.32
  121.7 0.0 copy-done
  121.7 4.6 %fusion.51 = bf16[1024,2048]{1,0:T(8,128)(2,1)} fusion(bf16[1,2048,768]{2,1,0:T(8,128)(2,1)S(1)} %copy-done, bf16[128,2048]{1,0:T(8,128)(2,1)} %bitcast.207, bf16[1,2048,768]{2,1,0:T(8,128)(2,1)} %param.10, f32[128,768]{1,0:T(8,128)} %fusion.46), kind=kOutput, calls=%fused_computation.51 | convolution fusion | flops 806158336 | bytes 7733248 | tf_op jit(solution)/shard_map/dot_general | solution.py:19
  126.2 4.6 %fusion.57 = bf16[1024,2048]{1,0:T(8,128)(2,1)} fusion(bf16[1024,2048]{1,0:T(8,128)(2,1)} %fusion.51, bf16[1,2048,768]{2,1,0:T(8,128)(2,1)S(1)} %copy-done, bf16[128,2048]{1,0:T(8,128)(2,1)} %bitcast.205, bf16[1,2048,768]{2,1,0:T(8,128)(2,1)} %param.10, f32[128,768]{1,0:T(8,128)} %fusion.44), kind=kOutput, calls=%fused_computation.53 | convolution fusion | flops 806158336 | bytes 7733248 | tf_op jit(solution)/shard_map/dot_general | solution.py:19
  130.8 4.6 %fusion.63 = bf16[1024,2048]{1,0:T(8,128)(2,1)} fusion(bf16[1024,2048]{1,0:T(8,128)(2,1)} %fusion.57, bf16[1,2048,768]{2,1,0:T(8,128)(2,1)S(1)} %copy-done, bf16[128,2048]{1,0:T(8,128)(2,1)} %bitcast.203, bf16[1,2048,768]{2,1,0:T(8,128)(2,1)} %param.10, f32[128,768]{1,0:T(8,128)} %fusion.42), kind=kOutput, calls=%fused_computation.55 | convolution fusion | flops 806158336 | bytes 7733248 | tf_op jit(solution)/shard_map/dot_general | solution.py:19
  135.4 4.6 %fusion.69 = bf16[1024,2048]{1,0:T(8,128)(2,1)} fusion(bf16[1024,2048]{1,0:T(8,128)(2,1)} %fusion.63, bf16[1,2048,768]{2,1,0:T(8,128)(2,1)S(1)} %copy-done, bf16[128,2048]{1,0:T(8,128)(2,1)} %bitcast.201, bf16[1,2048,768]{2,1,0:T(8,128)(2,1)} %param.10, f32[128,768]{1,0:T(8,128)} %fusion.40), kind=kOutput, calls=%fused_computation.57 | convolution fusion | flops 806158336 | bytes 7733248 | tf_op jit(solution)/shard_map/dot_general | solution.py:19
  140.0 4.6 %fusion.75 = bf16[1024,2048]{1,0:T(8,128)(2,1)} fusion(bf16[1024,2048]{1,0:T(8,128)(2,1)} %fusion.69, bf16[1,2048,768]{2,1,0:T(8,128)(2,1)S(1)} %copy-done, bf16[128,2048]{1,0:T(8,128)(2,1)} %bitcast.199, bf16[1,2048,768]{2,1,0:T(8,128)(2,1)} %param.10, f32[128,768]{1,0:T(8,128)} %fusion.38), kind=kOutput, calls=%fused_computation.59 | convolution fusion | flops 806158336 | bytes 7733248 | tf_op jit(solution)/shard_map/dot_general | solution.py:19
  144.5 4.6 %fusion.81 = bf16[1024,2048]{1,0:T(8,128)(2,1)} fusion(bf16[1024,2048]{1,0:T(8,128)(2,1)} %fusion.75, bf16[1,2048,768]{2,1,0:T(8,128)(2,1)S(1)} %copy-done, bf16[128,2048]{1,0:T(8,128)(2,1)} %bitcast.197, bf16[1,2048,768]{2,1,0:T(8,128)(2,1)} %param.10, f32[128,768]{1,0:T(8,128)} %fusion.36), kind=kOutput, calls=%fused_computation.61 | convolution fusion | flops 806158336 | bytes 7733248 | tf_op jit(solution)/shard_map/dot_general | solution.py:19
  149.1 4.8 %fusion.87 = bf16[1024,2048]{1,0:T(8,128)(2,1)} fusion(bf16[1024,2048]{1,0:T(8,128)(2,1)} %fusion.81, bf16[1,2048,768]{2,1,0:T(8,128)(2,1)S(1)} %copy-done, bf16[128,2048]{1,0:T(8,128)(2,1)} %bitcast.195, bf16[1,2048,768]{2,1,0:T(8,128)(2,1)} %param.10, f32[128,768]{1,0:T(8,128)} %fusion.34), kind=kOutput, calls=%fused_computation.63 | convolution fusion | flops 806158336 | bytes 7733248 | tf_op jit(solution)/shard_map/dot_general | solution.py:19
  153.9 4.5 %fusion.93 = bf16[1024,2048]{1,0:T(8,128)(2,1)} fusion(bf16[1024,2048]{1,0:T(8,128)(2,1)} %fusion.87, bf16[1,2048,768]{2,1,0:T(8,128)(2,1)S(1)} %copy-done, bf16[128,2048]{1,0:T(8,128)(2,1)} %bitcast.193, bf16[1,2048,768]{2,1,0:T(8,128)(2,1)} %param.10, f32[128,768]{1,0:T(8,128)S(1)} %fusion.32), kind=kOutput, calls=%fused_computation.65 | convolution fusion | flops 806158336 | bytes 7733248 | tf_op jit(solution)/shard_map/dot_general | solution.py:19
  158.4 0.0 copy-start.10
  158.4 5.3 %all-to-all-start.1 = ((bf16[16,64,2048]{2,1,0:T(8,128)(2,1)}), bf16[16,64,2048]{2,1,0:T(8,128)(2,1)}, u32[]{:S(2)}, u32[]{:S(2)}) async-start(bf16[16,64,2048]{2,1,0:T(8,128)(2,1)} %bitcast.191), calls=%async_computation.1 | async-start | bytes 8388608 | tf_op jit(solution)/shard_map/all_to_all | solution.py:48
  163.7 0.0 copy-done.10
  163.8 0.1 copy.11
  163.9 92.3 %all-to-all-done.1 = bf16[16,64,2048]{2,1,0:T(8,128)(2,1)} async-done(((bf16[16,64,2048]{2,1,0:T(8,128)(2,1)}), bf16[16,64,2048]{2,1,0:T(8,128)(2,1)}, u32[]{:S(2)}, u32[]{:S(2)}) %all-to-all-start.1) | async-done | bytes 4194336 | tf_op jit(solution)/shard_map/all_to_all | solution.py:48
  256.2 8.0 %gather_fusion = bf16[512,2048]{1,0:T(8,128)(2,1)} fusion(bf16[1024,2048]{1,0:T(8,128)(2,1)} %bitcast.17, s32[1024]{0:T(1024)S(1)} %pad_clamp_fusion), kind=kCustom, calls=%fused_computation | custom fusion | bytes 4196352 | tf_op jit(solution)/shard_map/gather | solution.py:51
  264.2 2.3 fusion.96
  266.5 0.9 copy.16
  (5 shorter events, 0.1 us)
Async XLA Ops:
  0.0 121.7 %copy-start = (bf16[1,2048,768]{2,1,0:T(8,128)(2,1)S(1)}, bf16[1,2048,768]{2,1,0:T(8,128)(2,1)}, u32[]{:S(2)}) copy-start(bf16[1,2048,768]{2,1,0:T(8,128)(2,1)} %param.11) | copy-start | bytes 9437188
  108.8 2.7 %copy-start.1 = (bf16[1,2048,768]{2,1,0:T(8,128)(2,1)S(1)}, bf16[1,2048,768]{2,1,0:T(8,128)(2,1)}, u32[]{:S(2)}) copy-start(bf16[1,2048,768]{2,1,0:T(8,128)(2,1)} %param.9) | copy-start | bytes 9437188
  109.4 4.9 %copy-start.8 = (bf16[2,64,2048]{2,1,0:T(8,128)(2,1)}, bf16[2,64,2048]{2,1,0:T(8,128)(2,1)S(1)}, u32[]{:S(2)}) copy-start(bf16[2,64,2048]{2,1,0:T(8,128)(2,1)S(1)} %get-tuple-element.11) | copy-start | bytes 1572868
  109.4 4.9 %copy-start.9 = (bf16[2,64,2048]{2,1,0:T(8,128)(2,1)}, bf16[2,64,2048]{2,1,0:T(8,128)(2,1)S(1)}, u32[]{:S(2)}) copy-start(bf16[2,64,2048]{2,1,0:T(8,128)(2,1)S(1)} %get-tuple-element.12) | copy-start | bytes 1572868
  109.4 4.9 %copy-start.7 = (bf16[2,64,2048]{2,1,0:T(8,128)(2,1)}, bf16[2,64,2048]{2,1,0:T(8,128)(2,1)S(1)}, u32[]{:S(2)}) copy-start(bf16[2,64,2048]{2,1,0:T(8,128)(2,1)S(1)} %get-tuple-element.10) | copy-start | bytes 1572868
  109.4 6.2 %copy-start.6 = (bf16[2,64,2048]{2,1,0:T(8,128)(2,1)}, bf16[2,64,2048]{2,1,0:T(8,128)(2,1)S(1)}, u32[]{:S(2)}) copy-start(bf16[2,64,2048]{2,1,0:T(8,128)(2,1)S(1)} %get-tuple-element.9) | copy-start | bytes 1572868
  109.4 7.5 %copy-start.5 = (bf16[2,64,2048]{2,1,0:T(8,128)(2,1)}, bf16[2,64,2048]{2,1,0:T(8,128)(2,1)S(1)}, u32[]{:S(2)}) copy-start(bf16[2,64,2048]{2,1,0:T(8,128)(2,1)S(1)} %get-tuple-element.8) | copy-start | bytes 1572868
  109.4 8.9 %copy-start.4 = (bf16[2,64,2048]{2,1,0:T(8,128)(2,1)}, bf16[2,64,2048]{2,1,0:T(8,128)(2,1)S(1)}, u32[]{:S(2)}) copy-start(bf16[2,64,2048]{2,1,0:T(8,128)(2,1)S(1)} %get-tuple-element.7) | copy-start | bytes 1572868
  109.5 10.2 %copy-start.3 = (bf16[2,64,2048]{2,1,0:T(8,128)(2,1)}, bf16[2,64,2048]{2,1,0:T(8,128)(2,1)S(1)}, u32[]{:S(2)}) copy-start(bf16[2,64,2048]{2,1,0:T(8,128)(2,1)S(1)} %get-tuple-element.6) | copy-start | bytes 1572868
  109.5 11.6 %copy-start.2 = (bf16[2,64,2048]{2,1,0:T(8,128)(2,1)}, bf16[2,64,2048]{2,1,0:T(8,128)(2,1)S(1)}, u32[]{:S(2)}) copy-start(bf16[2,64,2048]{2,1,0:T(8,128)(2,1)S(1)} %get-tuple-element.5) | copy-start | bytes 1572868
  158.4 5.4 %copy-start.10 = (f32[64,8]{0,1:T(8,128)S(1)}, f32[64,8]{0,1:T(8,128)}, u32[]{:S(2)}) copy-start(f32[64,8]{0,1:T(8,128)} %param.8) | copy-start | bytes 6148
  158.4 97.8 %all-to-all-start.1 = ((bf16[16,64,2048]{2,1,0:T(8,128)(2,1)}), bf16[16,64,2048]{2,1,0:T(8,128)(2,1)}, u32[]{:S(2)}, u32[]{:S(2)}) async-start(bf16[16,64,2048]{2,1,0:T(8,128)(2,1)} %bitcast.191), calls=%async_computation.1 | async-start | bytes 8388608 | tf_op jit(solution)/shard_map/all_to_all | solution.py:48
where the time goes:
time: 268 us; the launch traced here: 267 us
  blocking collectives  98.7 us (37%)
  waiting for transfers between devices  92.3 us (34%)
  matrix products  49.1 us (18%)
  local copies, waits for them, and re-layouts  19.7 us (7%)
  starting transfers between devices  5.35 us (2%)
    all_to_all x1, blocking collectives, body(): lax.all_to_all(send, 'expert', split_axis=0, concat_axis=0, tiled=True)  98.7 us
    all_to_all x1, waiting for transfers between devices, body(): lax.all_to_all(expert_out.reshape(experts, cap, width), 'expert', split_a...  92.3 us
    dot_general x8, matrix products, expert_rows(): lax.dot_general(hidden, down_w, (((1,), (1,)), ((), ())), preferred_eleme...  36.7 us
    dot_general x8, matrix products, expert_rows(): gate_val = jnp.dot(block_rows, gate_w, preferred_element_type=jnp.float32)  10.1 us
    gather x1, local copies, waits for them, and re-layouts, body(): picked = back.reshape(slots_all, width)[slot].reshape(tok_count, top, width)  8.01 us
    scatter x1, local copies, waits for them, and re-layouts, body(): jnp.zeros((slots_all, width), jnp.bfloat16).at[slot]  6.58 us
  transfers between devices with their start and end apart: 1, of which 1 were waited for; matrix products, arithmetic and copies ran while one was open for 0% of the time, Pallas kernels for 0%

commit v1 on v0

--- a/solution.py
+++ b/solution.py
@@ -23,11 +23,10 @@
     return jnp.concatenate(pieces, 0)
 
 
-def body(tokens, expert_ids, router_weights, w_gate, w_up, w_down):
+def routed_body(cap, tokens, expert_ids, router_weights, w_gate, w_up, w_down):
     tok_count, top = expert_ids.shape
     width = tokens.shape[1]
     experts = lax.axis_size("expert")
-    cap = max(2, min(tok_count, 2 * tok_count * top // experts))
     slots_all = experts * cap
     flat_ids = expert_ids.reshape(-1)
     onehot = (flat_ids[:, None] == jnp.arange(experts, dtype=jnp.int32)[None, :]).astype(jnp.int32)
@@ -53,6 +52,35 @@
     return mixed.astype(jnp.bfloat16)
 
 
+def dense_body(tokens, expert_ids, router_weights, w_gate, w_up, w_down):
+    experts = lax.axis_size("expert")
+    axes = ("expert", "dp") if lax.axis_size("dp") > 1 else "expert"
+    chosen = expert_ids[:, :, None] == jnp.arange(experts, dtype=jnp.int32)[None, None, :]
+    table = jnp.sum(jnp.where(chosen, router_weights[:, :, None], 0.0), 1)
+    table = lax.all_gather(table, axes, axis=0, tiled=True)
+    rows = lax.all_gather(tokens, axes, axis=0, tiled=True)
+    mine = jnp.arange(experts, dtype=jnp.int32)[None, :] == lax.axis_index("expert")
+    weight = jnp.sum(jnp.where(mine, table, 0.0), 1, keepdims=True)
+    gate_val = jnp.dot(rows, w_gate[0], preferred_element_type=jnp.float32)
+    up_val = jnp.dot(rows, w_up[0], preferred_element_type=jnp.float32)
+    hidden = (jax.nn.silu(gate_val) * up_val).astype(jnp.bfloat16)
+    out = lax.dot_general(
+        hidden, w_down[0], (((1,), (1,)), ((), ())), preferred_element_type=jnp.float32
+    )
+    part = (out * weight).astype(jnp.bfloat16)
+    return lax.psum_scatter(part, axes, scatter_dimension=0, tiled=True)
+
+
+def body(tokens, expert_ids, router_weights, w_gate, w_up, w_down):
+    tok_count, top = expert_ids.shape
+    experts = lax.axis_size("expert")
+    cap = max(2, min(tok_count, 2 * tok_count * top // experts))
+    args = (tokens, expert_ids, router_weights, w_gate, w_up, w_down)
+    if cap >= tok_count:
+        return dense_body(*args)
+    return routed_body(cap, *args)
+
+
 def solution(mesh):
     in_specs = (
         P(("parts", "expert", "dp"), None),

time: 268 us -> 162 us (0.60)
  the two profiles are of different devices: /device:TPU:11 before, /device:TPU:0 now
where the time goes in v1:
time: 162 us
  waiting for transfers between devices  103 us (64%)
  blocking collectives  23.6 us (15%)
  matrix products  20.7 us (13%)
  between operations  13.4 us (8%)
    reduce_scatter x1, waiting for transfers between devices, dense_body(): return lax.psum_scatter(part, axes, scatter_dimension=0, tiled=True)  71.5 us
    all_gather x1, waiting for transfers between devices, dense_body(): rows = lax.all_gather(tokens, axes, axis=0, tiled=True)  30.8 us
    all_gather x1, blocking collectives, dense_body(): table = lax.all_gather(table, axes, axis=0, tiled=True)  23.6 us
    dot_general x1, matrix products, dense_body(): lax.dot_general(hidden, w_down[0], (((1,), (1,)), ((), ())), preferred_el...  12.3 us
    dot_general x1, matrix products, dense_body(): up_val = jnp.dot(rows, w_up[0], preferred_element_type=jnp.float32)  8.33 us
  transfers between devices with their start and end apart: 2, of which 2 were waited for; matrix products, arithmetic and copies ran while one was open for 1% of the time, Pallas kernels for 0%

profile of v1, /device:TPU:0, one launch (start us, length us, event | category | flops | bytes accessed | tf_op | source)
XLA Modules:
  0.0 161.8 jit_solution(13165605166577742958)
XLA Ops:
  6.5 0.0 copy-start
  6.5 0.0 all-gather.3.cloned.1.call-start
  6.5 0.7 all-gather.3.cloned.1.call-update
  7.3 0.0 reduce-scatter.2.cloned.1.call-start
  7.3 0.9 select_reduce_fusion.1
  8.2 23.6 %all-gather = f32[16,64,16]{1,2,0:T(8,128)S(1)} all-gather(f32[1,64,16]{1,2,0:T(8,128)S(1)} %bitcast.18), channel_id=1, replica_groups=mesh['parts'=2,'expert'=16,'dp'=1] {'expert'}, dimensions={0}, use_global_device_ids=true | all-gather | bytes 69632 | tf_op jit(solution)/shard_map/all_gather | solution.py:60
  31.8 0.1 reshape.9
  31.9 0.1 select_reduce_fusion
  32.0 30.8 %all-gather.3.cloned.1.call-done = bf16[1024,2048]{1,0:T(8,128)(2,1)} async-done(((bf16[64,2048]{1,0:T(8,128)(2,1)}), bf16[1024,2048]{1,0:T(8,128)(2,1)}) %all-gather.3.cloned.1.call-update) | async-done | bytes 4194320 | tf_op jit(solution)/shard_map/all_gather | solution.py:61
  62.8 8.3 %fusion.1 = f32[1024,768]{1,0:T(8,128)} fusion(bf16[1024,2048]{1,0:T(8,128)(2,1)} %all-gather.3.cloned.1.call-done, bf16[1,2048,768]{2,1,0:T(8,128)(2,1)} %param.10), kind=kOutput, calls=%fused_computation.2 | convolution fusion | flops 3221225472 | bytes 10485760 | tf_op jit(solution)/shard_map/dot_general | solution.py:65
  71.1 0.0 copy-done
  71.1 12.3 %multiply_convert_fusion = bf16[1024,2048]{1,0:T(8,128)(2,1)} fusion(f32[1024]{0:T(1024)S(1)} %select_reduce_fusion, bf16[1,2048,768]{2,1,0:T(8,128)(2,1)S(1)} %copy-done, f32[1024,768]{1,0:T(8,128)} %fusion.1, bf16[1024,2048]{1,0:T(8,128)(2,1)} %all-gather.3.cloned.1.call-done, bf16[1,2048,768]{2,1,0:T(8,128)(2,1)} %param.9), kind=kOutput, calls=%fused_computation | convolution fusion | flops 6451363840 | bytes 17829888 | tf_op jit(solution)/shard_map/dot_general | solution.py:67
  83.5 0.0 reduce-scatter.2.cloned.1.call-update
  83.5 71.5 %reduce-scatter.2.cloned.1.call-done = bf16[64,2048]{1,0:T(8,128)(2,1)} async-done(((bf16[1024,2048]{1,0:T(8,128)(2,1)}), bf16[64,2048]{1,0:T(8,128)(2,1)}) %reduce-scatter.2.cloned.1.call-update) | async-done | bytes 262160 | tf_op jit(solution)/shard_map/reduce_scatter | solution.py:71
  (2 shorter events, 0.0 us)
Async XLA Ops:
  6.5 64.6 %copy-start = (bf16[1,2048,768]{2,1,0:T(8,128)(2,1)S(1)}, bf16[1,2048,768]{2,1,0:T(8,128)(2,1)}, u32[]{:S(2)}) copy-start(bf16[1,2048,768]{2,1,0:T(8,128)(2,1)} %param.11) | copy-start | bytes 9437188
  6.5 56.3 %all-gather.3.cloned.1.call-start = ((), (), s32[]{:S(2)}) async-start(), calls=%async_computation.1 | async-start | bytes 4456448 | tf_op jit(solution)/shard_map/all_gather | solution.py:61
  7.3 147.7 %reduce-scatter.2.cloned.1.call-start = ((), (), s32[]{:S(2)}) async-start(), calls=%async_computation.2 | async-start | bytes 4456448 | tf_op jit(solution)/shard_map/reduce_scatter | solution.py:71
Sparse Core Ops, SparseCore 0:
  9.5 53.2 all-gather.2
  83.6 71.2 reduce-scatter.1

commit v2 on v1

--- a/solution.py
+++ b/solution.py
@@ -1,9 +1,15 @@
+import functools
 import math
 
 import jax
 import jax.numpy as jnp
 from jax import lax
+from jax.experimental import pallas as pl
+from jax.experimental.pallas import tpu as pltpu
 from jax.sharding import PartitionSpec as P
+
+LANES = 128
+PARTS = 3
 
 
 def expert_rows(rows, gate_w, up_w, down_w):
@@ -71,11 +77,295 @@
     return lax.psum_scatter(part, axes, scatter_dimension=0, tiled=True)
 
 
+MESH = pl.DeviceIdType.MESH
+
+
+def fused_kernel(
+    depth,
+    ext_ref, gate_hbm, up_hbm, down_hbm, out_ref,
+    tok, gate_w, up_w, down_w, part, from_core, to_x, from_x, to_z, from_z,
+    load_sem, own_sem,
+    agz_send, agz_recv, agx_send, agx_recv, agc_send, agc_recv,
+    rsc_send, rsc_recv, rsx_send, rsx_recv, rsz_send, rsz_recv,
+):
+    me = lax.axis_index("expert")
+    core = lax.rem(me, 2)
+    col = lax.rem(me // 2, 2)
+    row = me // 4
+    width = out_ref.shape[1]
+    count = out_ref.shape[0]
+    ff = gate_w.shape[1]
+
+    def device(r, x, c):
+        return {"expert": (r * 2 + x) * 2 + c}
+
+    partner = device(row, col, 1 - core)
+    beside = device(row, 1 - col, core)
+    above = device(row + 1, col, core)
+    below = device(row - 1, col, core)
+
+    loads = [
+        pltpu.make_async_copy(gate_hbm.at[0], gate_w, load_sem.at[0]),
+        pltpu.make_async_copy(up_hbm.at[0], up_w, load_sem.at[1]),
+        pltpu.make_async_copy(down_hbm.at[0], down_w, load_sem.at[2]),
+    ]
+    own = pltpu.make_async_copy(ext_ref, tok.at[row, core, col], own_sem.at[0])
+
+    barrier = pltpu.get_barrier_semaphore()
+    for other in (partner, beside):
+        pl.semaphore_signal(barrier, inc=1, device_id=other, device_id_type=MESH)
+
+    @pl.when(row > 0)
+    def _():
+        pl.semaphore_signal(barrier, inc=1, device_id=below, device_id_type=MESH)
+
+    @pl.when(row < depth - 1)
+    def _():
+        pl.semaphore_signal(barrier, inc=1, device_id=above, device_id_type=MESH)
+
+    own.start()
+    for load in loads:
+        load.start()
+    pl.semaphore_wait(barrier, jnp.where((row > 0) & (row < depth - 1), 4, 3))
+
+    def remote(src, dst, send_sem, recv_sem, target):
+        return pltpu.make_async_remote_copy(
+            src_ref=src, dst_ref=dst, send_sem=send_sem, recv_sem=recv_sem,
+            device_id=target, device_id_type=MESH,
+        )
+
+    def gather_z(s, target, src=None):
+        block = tok.at[s, core, col]
+        way = 0 if target is above else 1
+        return remote(block if src is None else src, block, agz_send.at[s, way], agz_recv.at[s], target)
+
+    def gather_x(s, src=None):
+        block = tok.at[s, core, col]
+        return remote(block if src is None else src, block, agx_send.at[s], agx_recv.at[s], beside)
+
+    def gather_c(s, x, which, src=None):
+        block = tok.at[s, core, x]
+        return remote(block if src is None else src, block, agc_send.at[s, which], agc_recv.at[s, which], partner)
+
+    def reduce_c(s):
+        return remote(part.at[s, 1 - core], from_core.at[s], rsc_send.at[s], rsc_recv.at[s], partner)
+
+    def reduce_x(s):
+        return remote(to_x.at[s], from_x.at[s], rsx_send.at[s], rsx_recv.at[s], beside)
+
+    def reduce_z(s, target):
+        way = 0 if target is above else 1
+        return remote(to_z.at[s], from_z.at[way, s], rsz_send.at[s], rsz_recv.at[way, s], target)
+
+    @pl.when(row < depth - 1)
+    def _():
+        gather_z(row, above, ext_ref).start()
+
+    @pl.when(row > 0)
+    def _():
+        gather_z(row, below, ext_ref).start()
+
+    gather_x(row, ext_ref).start()
+    gather_c(row, col, 0, ext_ref).start()
+
+    def arrive_z(dist):
+        @pl.when(row - dist >= 0)
+        def _():
+            s = row - dist
+            gather_z(s, above).wait_recv()
+
+            @pl.when(row < depth - 1)
+            def _():
+                gather_z(s, above).start()
+
+            gather_x(s).start()
+            gather_c(s, col, 0).start()
+
+        @pl.when(row + dist < depth)
+        def _():
+            s = row + dist
+            gather_z(s, below).wait_recv()
+
+            @pl.when(row > 0)
+            def _():
+                gather_z(s, below).start()
+
+            gather_x(s).start()
+            gather_c(s, col, 0).start()
+
+    def slab(k):
+        low = jnp.where(row + k < depth, row + k, depth - 1 - k)
+        high = jnp.where(row - k >= 0, row - k, k)
+        return jnp.where(row < depth // 2, low, high)
+
+    lane = lax.broadcasted_iota(jnp.int32, (1, LANES), 1)
+    pick = jnp.where((lane % (depth * 4) == me) & (lane < PARTS * depth * 4), 1.0, 0.0)
+    block_cols = 512
+
+    def compute(s):
+        rows = tok[s].reshape(4 * count, width + LANES)
+        weight = jnp.sum(rows[:, width:].astype(jnp.float32) * pick, 1, keepdims=True)
+        rows = rows[:, :width]
+        gate_val = jnp.dot(rows, gate_w[...], preferred_element_type=jnp.float32)
+        up_val = jnp.dot(rows, up_w[...], preferred_element_type=jnp.float32)
+        hidden = (gate_val / (1.0 + jnp.exp(-gate_val)) * up_val).astype(jnp.bfloat16)
+        for at in range(0, width, block_cols):
+            value = lax.dot_general(
+                hidden, down_w[at : at + block_cols, :], (((1,), (1,)), ((), ())),
+                preferred_element_type=jnp.float32,
+            )
+            part[s, :, :, :, at : at + block_cols] = (
+                (value * weight).astype(jnp.bfloat16).reshape(2, 2, count, block_cols)
+            )
+
+    def reduce_over_core(s):
+        reduce_c(s).wait_recv()
+        total = part[s, core, 1 - col].astype(jnp.float32) + from_core[s, 1 - col].astype(jnp.float32)
+        to_x[s] = total.astype(jnp.bfloat16)
+        reduce_x(s).start()
+
+    def column_sum(s):
+        total = part[s, core, col].astype(jnp.float32) + from_core[s, col].astype(jnp.float32)
+        return total + from_x[s].astype(jnp.float32)
+
+    def send_z(s):
+        reduce_x(s).wait_recv()
+
+        def side(way, target, upstream):
+            @pl.when(upstream)
+            def _():
+                reduce_z(s, target).wait_recv()
+                total = column_sum(s) + from_z[way, s].astype(jnp.float32)
+                to_z[s] = total.astype(jnp.bfloat16)
+
+            @pl.when(jnp.logical_not(upstream))
+            def _():
+                to_z[s] = column_sum(s).astype(jnp.bfloat16)
+
+            reduce_z(s, target).start()
+
+        @pl.when(s > row)
+        def _():
+            side(0, above, row > 0)
+
+        @pl.when(s < row)
+        def _():
+            side(1, below, row < depth - 1)
+
+    own.wait()
+    for k in range(depth):
+        s = slab(k)
+        if k + 1 < depth:
+            arrive_z(k + 1)
+        gather_x(s).wait_recv()
+        gather_c(s, 1 - col, 1).start()
+        gather_c(s, col, 0).wait_recv()
+        gather_c(s, 1 - col, 1).wait_recv()
+        if k == 0:
+            for load in loads:
+                load.wait()
+        compute(s)
+        reduce_c(s).start()
+        if k >= 1:
+            reduce_over_core(slab(k - 1))
+    reduce_over_core(slab(depth - 1))
+    for k in range(1, depth):
+        send_z(slab(k))
+
+    reduce_x(row).wait_recv()
+    @pl.when(row < depth - 1)
+    def _():
+        reduce_z(row, below).wait_recv()
+
+    @pl.when(row > 0)
+    def _():
+        reduce_z(row, above).wait_recv()
+
+    @pl.when(row == 0)
+    def _():
+        out_ref[...] = (column_sum(row) + from_z[1, row].astype(jnp.float32)).astype(jnp.bfloat16)
+
+    @pl.when(row == depth - 1)
+    def _():
+        out_ref[...] = (column_sum(row) + from_z[0, row].astype(jnp.float32)).astype(jnp.bfloat16)
+
+    @pl.when((row > 0) & (row < depth - 1))
+    def _():
+        both = from_z[0, row].astype(jnp.float32) + from_z[1, row].astype(jnp.float32)
+        out_ref[...] = (column_sum(row) + both).astype(jnp.bfloat16)
+
+    for s in range(depth):
+        gather_x(s).wait_send()
+        gather_c(s, col, 0).wait_send()
+        gather_c(s, col, 1).wait_send()
+        reduce_c(s).wait_send()
+        reduce_x(s).wait_send()
+
+        @pl.when(row != s)
+        def _():
+            reduce_z(s, above).wait_send()
+
+        @pl.when((row >= s) & (row < depth - 1))
+        def _():
+            gather_z(s, above).wait_send()
+
+        @pl.when((row <= s) & (row > 0))
+        def _():
+            gather_z(s, below).wait_send()
+
+
+def fused_body(tokens, expert_ids, router_weights, w_gate, w_up, w_down):
+    experts = lax.axis_size("expert")
+    depth = experts // 4
+    count, width = tokens.shape
+    ff = w_gate.shape[2]
+    chosen = expert_ids[:, :, None] == jnp.arange(experts, dtype=jnp.int32)[None, None, :]
+    left = jnp.sum(jnp.where(chosen, router_weights[:, :, None], 0.0), 1)
+    terms = []
+    for _ in range(PARTS):
+        term = lax.reduce_precision(left, 8, 7)
+        left = left - term
+        terms.append(term.astype(jnp.bfloat16))
+    pad = jnp.zeros((count, LANES - PARTS * experts), jnp.bfloat16)
+    ext = jnp.concatenate([tokens] + terms + [pad], 1)
+    wide = width + LANES
+    bf16 = jnp.bfloat16
+    dma = pltpu.SemaphoreType.DMA
+    return pl.pallas_call(
+        functools.partial(fused_kernel, depth),
+        out_shape=jax.ShapeDtypeStruct((count, width), bf16),
+        in_specs=[pl.BlockSpec(memory_space=pltpu.VMEM)] + [pl.BlockSpec(memory_space=pl.ANY)] * 3,
+        out_specs=pl.BlockSpec(memory_space=pltpu.VMEM),
+        scratch_shapes=[
+            pltpu.VMEM((depth, 2, 2, count, wide), bf16),
+            pltpu.VMEM((width, ff), bf16),
+            pltpu.VMEM((width, ff), bf16),
+            pltpu.VMEM((width, ff), bf16),
+            pltpu.VMEM((depth, 2, 2, count, width), bf16),
+            pltpu.VMEM((depth, 2, count, width), bf16),
+            pltpu.VMEM((depth, count, width), bf16),
+            pltpu.VMEM((depth, count, width), bf16),
+            pltpu.VMEM((depth, count, width), bf16),
+            pltpu.VMEM((2, depth, count, width), bf16),
+            dma((3,)), dma((1,)),
+            dma((depth, 2)), dma((depth,)), dma((depth,)), dma((depth,)), dma((depth, 2)), dma((depth, 2)),
+            dma((depth,)), dma((depth,)), dma((depth,)), dma((depth,)), dma((depth,)), dma((2, depth)),
+        ],
+        compiler_params=pltpu.CompilerParams(
+            collective_id=0, has_side_effects=True, vmem_limit_bytes=60 * 1024 * 1024
+        ),
+        name="moe",
+    )(ext, w_gate, w_up, w_down)
+
+
 def body(tokens, expert_ids, router_weights, w_gate, w_up, w_down):
     tok_count, top = expert_ids.shape
     experts = lax.axis_size("expert")
     cap = max(2, min(tok_count, 2 * tok_count * top // experts))
     args = (tokens, expert_ids, router_weights, w_gate, w_up, w_down)
+    grid = experts % 4 == 0 and 8 <= experts <= 16 and lax.axis_size("dp") == 1
+    if cap >= tok_count and grid:
+        return fused_body(*args)
     if cap >= tok_count:
         return dense_body(*args)
     return routed_body(cap, *args)

time: 162 us -> 80.8 us (0.50)
  waiting for transfers between devices: 103 us -> 0 us
  Pallas kernels: 0 us -> 76.2 us
  blocking collectives: 23.6 us -> 0 us
  matrix products: 20.7 us -> 0 us
  between operations: 13.4 us -> 0.03 us
  local copies, waits for them, and re-layouts: 0.15 us -> 3.59 us
    pallas_call x0 -> x1, Pallas kernels: none -> 76.2 us  [fused_body(): pl.pallas_call(functools.partial(fused_kernel, depth), out_shape=jax.Shap...]
    reduce_scatter x1 -> x0, waiting for transfers between devices: 71.5 us -> none  [dense_body(): return lax.psum_scatter(part, axes, scatter_dimension=0, tiled=True)]
    all_gather x1 -> x0, waiting for transfers between devices: 30.8 us -> none  [dense_body(): rows = lax.all_gather(tokens, axes, axis=0, tiled=True)]
    all_gather x1 -> x0, blocking collectives: 23.6 us -> none  [dense_body(): table = lax.all_gather(table, axes, axis=0, tiled=True)]
    dot_general x2 -> x0, matrix products: 20.7 us -> none  [the longest x1 12.3 us: dense_body(): lax.dot_general(hidden, w_down[0], (((1,), (1,)), ((), ())), preferred_el...]
    concatenate x0 -> x1, local copies, waits for them, and re-layouts: none -> 1.75 us  [fused_body(): ext = jnp.concatenate([tokens] + terms + [pad], 1)]
  transfers between devices with their start and end apart: 2 -> 0, of which waited for: 2 -> 0; matrix products, arithmetic and copies ran while one was open for 1% -> 0% of each run, Pallas kernels for 0% -> 0%
where the time goes in v2:
time: 80.8 us; the launch traced here: 80.5 us
  Pallas kernels  76.2 us (94%)
  local copies, waits for them, and re-layouts  3.59 us (4%)
    pallas_call x1, Pallas kernels, fused_body(): pl.pallas_call(functools.partial(fused_kernel, depth), out_shape=jax.Shap...  76.2 us
    concatenate x1, local copies, waits for them, and re-layouts, fused_body(): ext = jnp.concatenate([tokens] + terms + [pad], 1)  1.75 us
    unnamed x1, local copies, waits for them, and re-layouts  1.67 us

profile of v2, /device:TPU:0, one launch (start us, length us, event | category | flops | bytes accessed | tf_op | source)
XLA Modules:
  0.0 80.5 jit_solution(5288027499867341990)
XLA Ops:
  0.0 0.7 select_reduce_fusion
  0.7 0.1 copy.12
  0.8 0.1 copy.11
  0.9 1.7 %concatenate.3.ext_ref = bf16[64,2176]{1,0:T(8,128)(2,1)} concatenate(bf16[64,2048]{1,0:T(8,128)(2,1)} %param.6, bf16[64,16]{1,0:T(8,128)(2,1)S(1)} %get-tuple-element.7, bf16[64,16]{1,0:T(8,128)(2,1)S(1)} %get-tuple-element.6, bf16[64,16]{1,0:T(8,128)(2,1)S(1)} %get-tuple-element.5, bf16[64,80]{1,0:T(8,128)(2,1)S(1)} %broadcast_in_dim.20), dimensions={1} | concatenate | bytes 557056 | tf_op jit(solution)/shard_map/concatenate | solution.py:330
  2.7 76.2 %moe.1 = bf16[64,2048]{1,0:T(8,128)(2,1)} custom-call(bf16[64,2176]{1,0:T(8,128)(2,1)} %concatenate.3.ext_ref, bf16[1,2048,768]{2,1,0:T(8,128)(2,1)} %gate_hbm.1, bf16[1,2048,768]{2,1,0:T(8,128)(2,1)} %up_hbm.1, bf16[1,2048,768]{2,1,0:T(8,128)(2,1)} %down_hbm.1), custom_call_target="tpu_custom_call" | custom-call | tf_op jit(solution)/shard_map/moe/pallas_call | solution.py:334
  78.9 1.7 %copy.15 = bf16[64,2048]{1,0:T(8,128)(2,1)} copy(bf16[64,2048]{1,0:T(8,128)(2,1)} %moe.1) | data formatting | bytes 524288
  (3 shorter events, 0.0 us)

commit v3 on v2

--- a/solution.py
+++ b/solution.py
@@ -78,6 +78,9 @@
 
 
 MESH = pl.DeviceIdType.MESH
+CHUNKS = 4
+X_FIRST = (0, 1, 2, 3)
+Z_FIRST = ()
 
 
 def fused_kernel(
@@ -150,12 +153,15 @@
     def reduce_c(s):
         return remote(part.at[s, 1 - core], from_core.at[s], rsc_send.at[s], rsc_recv.at[s], partner)
 
-    def reduce_x(s):
-        return remote(to_x.at[s], from_x.at[s], rsx_send.at[s], rsx_recv.at[s], beside)
-
-    def reduce_z(s, target):
+    def reduce_x(s, q):
+        return remote(to_x.at[s, q], from_x.at[s, q], rsx_send.at[s, q], rsx_recv.at[s, q], beside)
+
+    def reduce_z(s, q, target):
         way = 0 if target is above else 1
-        return remote(to_z.at[s], from_z.at[way, s], rsz_send.at[s], rsz_recv.at[way, s], target)
+        src, dst = to_z.at[s, q], from_z.at[way, s, q]
+        if q in X_FIRST:
+            src, dst = src.at[0], dst.at[0]
+        return remote(src, dst, rsz_send.at[s, q], rsz_recv.at[way, s, q], target)
 
     @pl.when(row < depth - 1)
     def _():
@@ -218,31 +224,67 @@
                 (value * weight).astype(jnp.bfloat16).reshape(2, 2, count, block_cols)
             )
 
+    cols = width // CHUNKS
+
+    def core_sum(s, x, q):
+        at = pl.ds(q * cols, cols)
+        return part[s, core, x, :, at].astype(jnp.float32) + from_core[s, x, :, at].astype(jnp.float32)
+
+    def column_sum(s, q):
+        return core_sum(s, col, q) + from_x[s, q].astype(jnp.float32)
+
+    def send_both(s, q, way, target, upstream):
+        for x in range(2):
+            total = core_sum(s, x, q)
+            if upstream:
+                total = total + from_z[way, s, q, x].astype(jnp.float32)
+            to_z[s, q, x] = total.astype(jnp.bfloat16)
+        reduce_z(s, q, target).start()
+
     def reduce_over_core(s):
         reduce_c(s).wait_recv()
-        total = part[s, core, 1 - col].astype(jnp.float32) + from_core[s, 1 - col].astype(jnp.float32)
-        to_x[s] = total.astype(jnp.bfloat16)
-        reduce_x(s).start()
-
-    def column_sum(s):
-        total = part[s, core, col].astype(jnp.float32) + from_core[s, col].astype(jnp.float32)
-        return total + from_x[s].astype(jnp.float32)
+        for q in X_FIRST:
+            to_x[s, q] = core_sum(s, 1 - col, q).astype(jnp.bfloat16)
+            reduce_x(s, q).start()
+
+        @pl.when((s > row) & (row == 0))
+        def _():
+            for q in Z_FIRST:
+                send_both(s, q, 0, above, False)
+
+        @pl.when((s < row) & (row == depth - 1))
+        def _():
+            for q in Z_FIRST:
+                send_both(s, q, 1, below, False)
+
+    def send_early(s):
+        def side(target):
+            for q in X_FIRST:
+                reduce_x(s, q).wait_recv()
+                to_z[s, q, 0] = column_sum(s, q).astype(jnp.bfloat16)
+                reduce_z(s, q, target).start()
+
+        @pl.when((s > row) & (row == 0))
+        def _():
+            side(above)
+
+        @pl.when((s < row) & (row == depth - 1))
+        def _():
+            side(below)
 
     def send_z(s):
-        reduce_x(s).wait_recv()
-
         def side(way, target, upstream):
             @pl.when(upstream)
             def _():
-                reduce_z(s, target).wait_recv()
-                total = column_sum(s) + from_z[way, s].astype(jnp.float32)
-                to_z[s] = total.astype(jnp.bfloat16)
-
-            @pl.when(jnp.logical_not(upstream))
-            def _():
-                to_z[s] = column_sum(s).astype(jnp.bfloat16)
-
-            reduce_z(s, target).start()
+                for q in Z_FIRST:
+                    reduce_z(s, q, target).wait_recv()
+                    send_both(s, q, way, target, True)
+                for q in X_FIRST:
+                    reduce_x(s, q).wait_recv()
+                    reduce_z(s, q, target).wait_recv()
+                    total = column_sum(s, q) + from_z[way, s, q, 0].astype(jnp.float32)
+                    to_z[s, q, 0] = total.astype(jnp.bfloat16)
+                    reduce_z(s, q, target).start()
 
         @pl.when(s > row)
         def _():
@@ -251,6 +293,29 @@
         @pl.when(s < row)
         def _():
             side(1, below, row < depth - 1)
+
+    def finish(ways):
+        def arrived(q, x):
+            total = from_z[ways[0], row, q, x].astype(jnp.float32)
+            for way in ways[1:]:
+                total = total + from_z[way, row, q, x].astype(jnp.float32)
+            return total
+
+        for q in Z_FIRST + X_FIRST:
+            for way in ways:
+                reduce_z(row, q, above if way == 0 else below).wait_recv()
+            at = pl.ds(q * cols, cols)
+            if q in Z_FIRST:
+                total = core_sum(row, 1 - col, q) + arrived(q, 1 - col)
+                to_x[row, q] = total.astype(jnp.bfloat16)
+                reduce_x(row, q).start()
+            else:
+                reduce_x(row, q).wait_recv()
+                out_ref[:, at] = (column_sum(row, q) + arrived(q, 0)).astype(jnp.bfloat16)
+        for q in Z_FIRST:
+            at = pl.ds(q * cols, cols)
+            reduce_x(row, q).wait_recv()
+            out_ref[:, at] = (column_sum(row, q) + arrived(q, col)).astype(jnp.bfloat16)
 
     own.wait()
     for k in range(depth):
@@ -266,44 +331,46 @@
                 load.wait()
         compute(s)
         reduce_c(s).start()
-        if k >= 1:
+        if k >= 2:
             reduce_over_core(slab(k - 1))
+        if k >= 3:
+            send_early(slab(k - 2))
     reduce_over_core(slab(depth - 1))
+    reduce_over_core(row)
     for k in range(1, depth):
+        if k >= depth - 2:
+            send_early(slab(k))
         send_z(slab(k))
 
-    reduce_x(row).wait_recv()
-    @pl.when(row < depth - 1)
-    def _():
-        reduce_z(row, below).wait_recv()
-
-    @pl.when(row > 0)
-    def _():
-        reduce_z(row, above).wait_recv()
-
     @pl.when(row == 0)
     def _():
-        out_ref[...] = (column_sum(row) + from_z[1, row].astype(jnp.float32)).astype(jnp.bfloat16)
+        finish((1,))
 
     @pl.when(row == depth - 1)
     def _():
-        out_ref[...] = (column_sum(row) + from_z[0, row].astype(jnp.float32)).astype(jnp.bfloat16)
+        finish((0,))
 
     @pl.when((row > 0) & (row < depth - 1))
     def _():
-        both = from_z[0, row].astype(jnp.float32) + from_z[1, row].astype(jnp.float32)
-        out_ref[...] = (column_sum(row) + both).astype(jnp.bfloat16)
+        finish((0, 1))
 
     for s in range(depth):
         gather_x(s).wait_send()
         gather_c(s, col, 0).wait_send()
         gather_c(s, col, 1).wait_send()
         reduce_c(s).wait_send()
-        reduce_x(s).wait_send()
+        for q in X_FIRST:
+            reduce_x(s, q).wait_send()
+
+        @pl.when(row == s)
+        def _():
+            for q in Z_FIRST:
+                reduce_x(s, q).wait_send()
 
         @pl.when(row != s)
         def _():
-            reduce_z(s, above).wait_send()
+            for q in range(CHUNKS):
+                reduce_z(s, q, above).wait_send()
 
         @pl.when((row >= s) & (row < depth - 1))
         def _():
@@ -343,13 +410,13 @@
             pltpu.VMEM((width, ff), bf16),
             pltpu.VMEM((depth, 2, 2, count, width), bf16),
             pltpu.VMEM((depth, 2, count, width), bf16),
-            pltpu.VMEM((depth, count, width), bf16),
-            pltpu.VMEM((depth, count, width), bf16),
-            pltpu.VMEM((depth, count, width), bf16),
-            pltpu.VMEM((2, depth, count, width), bf16),
+            pltpu.VMEM((depth, CHUNKS, count, width // CHUNKS), bf16),
+            pltpu.VMEM((depth, CHUNKS, count, width // CHUNKS), bf16),
+            pltpu.VMEM((depth, CHUNKS, 2, count, width // CHUNKS), bf16),
+            pltpu.VMEM((2, depth, CHUNKS, 2, count, width // CHUNKS), bf16),
             dma((3,)), dma((1,)),
             dma((depth, 2)), dma((depth,)), dma((depth,)), dma((depth,)), dma((depth, 2)), dma((depth, 2)),
-            dma((depth,)), dma((depth,)), dma((depth,)), dma((depth,)), dma((depth,)), dma((2, depth)),
+            dma((depth,)), dma((depth,)), dma((depth, CHUNKS)), dma((depth, CHUNKS)), dma((depth, CHUNKS)), dma((2, depth, CHUNKS)),
         ],
         compiler_params=pltpu.CompilerParams(
             collective_id=0, has_side_effects=True, vmem_limit_bytes=60 * 1024 * 1024

time: 80.8 us -> 68.7 us (0.85)
  Pallas kernels: 76.2 us -> 64.1 us
    pallas_call x1, Pallas kernels: 76.2 us -> 64.1 us  [fused_body(): pl.pallas_call(functools.partial(fused_kernel, depth), out_shape=jax.Shap...]
where the time goes in v3:
time: 68.7 us; the launch traced here: 68.4 us
  Pallas kernels  64.1 us (93%)
  local copies, waits for them, and re-layouts  3.59 us (5%)
  other arithmetic  0.74 us (1%)
    pallas_call x1, Pallas kernels, fused_body(): pl.pallas_call(functools.partial(fused_kernel, depth), out_shape=jax.Shap...  64.1 us
    concatenate x1, local copies, waits for them, and re-layouts, fused_body(): ext = jnp.concatenate([tokens] + terms + [pad], 1)  1.75 us
    unnamed x1, local copies, waits for them, and re-layouts  1.67 us

profile of v3, /device:TPU:0, one launch (start us, length us, event | category | flops | bytes accessed | tf_op | source)
XLA Modules:
  0.0 68.4 jit_solution(15457013585147881225)
XLA Ops:
  0.0 0.7 %select_reduce_fusion = f32[64,16]{0,1:T(8,128)S(1)} fusion(f32[64,8]{0,1:T(8,128)} %param.8, s32[64,8]{0,1:T(8,128)} %param.7), kind=kLoop, calls=%fused_computation | loop fusion | flops 23552 | bytes 8192 | tf_op jit(solution)/shard_map/reduce_sum | solution.py:390
  0.7 0.1 copy.12
  0.8 0.1 copy.11
  0.9 1.7 %concatenate.3.ext_ref = bf16[64,2176]{1,0:T(8,128)(2,1)} concatenate(bf16[64,2048]{1,0:T(8,128)(2,1)} %param.6, bf16[64,16]{1,0:T(8,128)(2,1)S(1)} %get-tuple-element.7, bf16[64,16]{1,0:T(8,128)(2,1)S(1)} %get-tuple-element.6, bf16[64,16]{1,0:T(8,128)(2,1)S(1)} %get-tuple-element.5, bf16[64,80]{1,0:T(8,128)(2,1)S(1)} %broadcast_in_dim.20), dimensions={1} | concatenate | bytes 557056 | tf_op jit(solution)/shard_map/concatenate | solution.py:397
  2.7 64.1 %moe.1 = bf16[64,2048]{1,0:T(8,128)(2,1)} custom-call(bf16[64,2176]{1,0:T(8,128)(2,1)} %concatenate.3.ext_ref, bf16[1,2048,768]{2,1,0:T(8,128)(2,1)} %gate_hbm.1, bf16[1,2048,768]{2,1,0:T(8,128)(2,1)} %up_hbm.1, bf16[1,2048,768]{2,1,0:T(8,128)(2,1)} %down_hbm.1), custom_call_target="tpu_custom_call" | custom-call | tf_op jit(solution)/shard_map/moe/pallas_call | solution.py:401
  66.8 1.7 %copy.15 = bf16[64,2048]{1,0:T(8,128)(2,1)} copy(bf16[64,2048]{1,0:T(8,128)(2,1)} %moe.1) | data formatting | bytes 524288
  (3 shorter events, 0.0 us)

commit v4 on v3

--- a/solution.py
+++ b/solution.py
@@ -85,7 +85,7 @@
 
 def fused_kernel(
     depth,
-    ext_ref, gate_hbm, up_hbm, down_hbm, out_ref,
+    token_ref, table_ref, gate_hbm, up_hbm, down_hbm, out_ref,
     tok, gate_w, up_w, down_w, part, from_core, to_x, from_x, to_z, from_z,
     load_sem, own_sem,
     agz_send, agz_recv, agx_send, agx_recv, agc_send, agc_recv,
@@ -112,7 +112,14 @@
         pltpu.make_async_copy(up_hbm.at[0], up_w, load_sem.at[1]),
         pltpu.make_async_copy(down_hbm.at[0], down_w, load_sem.at[2]),
     ]
-    own = pltpu.make_async_copy(ext_ref, tok.at[row, core, col], own_sem.at[0])
+    owns = [
+        pltpu.make_async_copy(
+            token_ref, tok.at[row, core, col, :, pl.ds(0, width)], own_sem.at[0]
+        ),
+        pltpu.make_async_copy(
+            table_ref, tok.at[row, core, col, :, pl.ds(width, LANES)], own_sem.at[1]
+        ),
+    ]
 
     barrier = pltpu.get_barrier_semaphore()
     for other in (partner, beside):
@@ -126,7 +133,8 @@
     def _():
         pl.semaphore_signal(barrier, inc=1, device_id=above, device_id_type=MESH)
 
-    own.start()
+    for own in owns:
+        own.start()
     for load in loads:
         load.start()
     pl.semaphore_wait(barrier, jnp.where((row > 0) & (row < depth - 1), 4, 3))
@@ -163,16 +171,19 @@
             src, dst = src.at[0], dst.at[0]
         return remote(src, dst, rsz_send.at[s, q], rsz_recv.at[way, s, q], target)
 
+    for own in owns:
+        own.wait()
+
     @pl.when(row < depth - 1)
     def _():
-        gather_z(row, above, ext_ref).start()
+        gather_z(row, above).start()
 
     @pl.when(row > 0)
     def _():
-        gather_z(row, below, ext_ref).start()
-
-    gather_x(row, ext_ref).start()
-    gather_c(row, col, 0, ext_ref).start()
+        gather_z(row, below).start()
+
+    gather_x(row).start()
+    gather_c(row, col, 0).start()
 
     def arrive_z(dist):
         @pl.when(row - dist >= 0)
@@ -317,7 +328,6 @@
             reduce_x(row, q).wait_recv()
             out_ref[:, at] = (column_sum(row, q) + arrived(q, col)).astype(jnp.bfloat16)
 
-    own.wait()
     for k in range(depth):
         s = slab(k)
         if k + 1 < depth:
@@ -394,14 +404,14 @@
         left = left - term
         terms.append(term.astype(jnp.bfloat16))
     pad = jnp.zeros((count, LANES - PARTS * experts), jnp.bfloat16)
-    ext = jnp.concatenate([tokens] + terms + [pad], 1)
+    table = jnp.concatenate(terms + [pad], 1)
     wide = width + LANES
     bf16 = jnp.bfloat16
     dma = pltpu.SemaphoreType.DMA
     return pl.pallas_call(
         functools.partial(fused_kernel, depth),
         out_shape=jax.ShapeDtypeStruct((count, width), bf16),
-        in_specs=[pl.BlockSpec(memory_space=pltpu.VMEM)] + [pl.BlockSpec(memory_space=pl.ANY)] * 3,
+        in_specs=[pl.BlockSpec(memory_space=pl.ANY)] * 5,
         out_specs=pl.BlockSpec(memory_space=pltpu.VMEM),
         scratch_shapes=[
             pltpu.VMEM((depth, 2, 2, count, wide), bf16),
@@ -414,7 +424,7 @@
             pltpu.VMEM((depth, CHUNKS, count, width // CHUNKS), bf16),
             pltpu.VMEM((depth, CHUNKS, 2, count, width // CHUNKS), bf16),
             pltpu.VMEM((2, depth, CHUNKS, 2, count, width // CHUNKS), bf16),
-            dma((3,)), dma((1,)),
+            dma((3,)), dma((2,)),
             dma((depth, 2)), dma((depth,)), dma((depth,)), dma((depth,)), dma((depth, 2)), dma((depth, 2)),
             dma((depth,)), dma((depth,)), dma((depth, CHUNKS)), dma((depth, CHUNKS)), dma((depth, CHUNKS)), dma((2, depth, CHUNKS)),
         ],
@@ -422,7 +432,7 @@
             collective_id=0, has_side_effects=True, vmem_limit_bytes=60 * 1024 * 1024
         ),
         name="moe",
-    )(ext, w_gate, w_up, w_down)
+    )(tokens, table, w_gate, w_up, w_down)
 
 
 def body(tokens, expert_ids, router_weights, w_gate, w_up, w_down):

time: 68.7 us -> 68.4 us (level)
  local copies, waits for them, and re-layouts: 3.59 us -> 1.92 us
  Pallas kernels: 64.1 us -> 64.8 us
  other arithmetic: 0.74 us -> 1.43 us
    concatenate x1, local copies, waits for them, and re-layouts: 1.75 us -> 0.08 us  [fused_body(): table = jnp.concatenate(terms + [pad], 1)]
    pallas_call x1, Pallas kernels: 64.1 us -> 64.8 us  [fused_body(): pl.pallas_call(functools.partial(fused_kernel, depth), out_shape=jax.Shap...]
    concatenate x0 -> x1, other arithmetic: none -> 0.69 us  [fused_body(): table = jnp.concatenate(terms + [pad], 1)]
where the time goes in v4:
time: 68.4 us; the launch traced here: 68.2 us
  Pallas kernels  64.8 us (95%)
  local copies, waits for them, and re-layouts  1.92 us (3%)
  other arithmetic  1.43 us (2%)
    pallas_call x1, Pallas kernels, fused_body(): pl.pallas_call(functools.partial(fused_kernel, depth), out_shape=jax.Shap...  64.8 us
    unnamed x1, local copies, waits for them, and re-layouts  1.67 us

profile of v4, /device:TPU:0, one launch (start us, length us, event | category | flops | bytes accessed | tf_op | source)
XLA Modules:
  0.0 68.2 jit_solution(17440046087187228008)
XLA Ops:
  0.0 0.1 pad.3.clone
  0.1 0.7 %select_reduce_fusion = f32[64,16]{0,1:T(8,128)S(1)} fusion(f32[64,8]{0,1:T(8,128)} %param.8, s32[64,8]{0,1:T(8,128)} %param.7), kind=kLoop, calls=%fused_computation | loop fusion | flops 23552 | bytes 8192 | tf_op jit(solution)/shard_map/reduce_sum | solution.py:400
  0.8 0.1 copy.12
  0.9 0.1 copy.11
  1.0 0.7 %maximum_maximum_fusion.table_ref = bf16[64,128]{1,0:T(8,128)(2,1)} fusion(bf16[64,16]{1,0:T(8,128)(2,1)S(1)} %get-tuple-element.6, bf16[64,16]{1,0:T(8,128)(2,1)S(1)} %get-tuple-element.5, bf16[64,16]{1,0:T(8,128)(2,1)S(1)} %get-tuple-element.7, bf16[128]{0:T(256)(128)(2,1)S(1)} %pad.3.clone), kind=kLoop, calls=%fused_computation.6 | loop fusion | flops 65536 | bytes 22784 | tf_op jit(solution)/shard_map/concatenate | solution.py:407
  1.7 64.8 %moe.1 = bf16[64,2048]{1,0:T(8,128)(2,1)} custom-call(bf16[64,2048]{1,0:T(8,128)(2,1)} %token_ref.1, bf16[64,128]{1,0:T(8,128)(2,1)} %maximum_maximum_fusion.table_ref, bf16[1,2048,768]{2,1,0:T(8,128)(2,1)} %gate_hbm.1, bf16[1,2048,768]{2,1,0:T(8,128)(2,1)} %up_hbm.1, bf16[1,2048,768]{2,1,0:T(8,128)(2,1)} %down_hbm.1), custom_call_target="tpu_custom_call" | custom-call | tf_op jit(solution)/shard_map/moe/pallas_call | solution.py:411
  66.5 1.7 %copy.15 = bf16[64,2048]{1,0:T(8,128)(2,1)} copy(bf16[64,2048]{1,0:T(8,128)(2,1)} %moe.1) | data formatting | bytes 524288
  (3 shorter events, 0.0 us)
